TPU v7x, 256 devices: a whole 4x4x8 slice. The times are simulated.
256 devices in a mesh: row: 8 (over x, y_lo), col: 32 (over z, y_hi, core).
Axes of the slice: x: 4, y: 4 (y_hi: 2, y_lo: 2; y = y_hi * 2 + y_lo), z: 8, core: 2. Of those that a mesh axis runs over, the one named last changes fastest.
Arguments:
- ancestor_inverse: float32 [16384, 16384], P('row', 'col'), may hold values from -6 to 6
- panel: float32 [6, 64, 256, 256], P(None, 'row', 'col'), may hold values from -0.0625 to 0.0625
- diag_inverse: float32 [6, 256, 256], replicated, as said below
- structure: int32 [6, 32], replicated, may hold values from 0 to 63, as said below
- block_slot: int32 [64], replicated, may hold values from 0 to 63, as said below
Outputs:
- off_block: float32 [6, 64, 256, 256], P(None, 'row', 'col')
- diag_block: float32 [6, 256, 256], replicated
Inputs may be any that keep to these rules, and one draw needn't show every extreme that they name: `structure`: the 32 entries of a supernode are distinct global row blocks. Mapped through block_slot, at most 6 of them fall into any aligned run of 8 storage slots, and for every supernode some run holds exactly 6. `block_slot`: A permutation of the 64 row blocks. `diag_inverse`: lower triangular with a positive diagonal.
All inputs are finite; a program needn't handle non-finite values.
Results may differ from a plain program's by a relative error of at most 0.0001.
Values sent between devices are 32-bit elements; how exact they have to be, the bound alone decides.
A program may use at most 128 MiB of HBM per device.

v0:
```python
import jax
import jax.numpy as jnp
from jax import lax
from jax.sharding import PartitionSpec as P


def spread(block, axis, owner):
    block = jnp.where(lax.axis_index(axis) == owner, block, jnp.zeros_like(block))
    return lax.psum(block, axis)


def gather_rows(normalized):
    return lax.all_gather(normalized, "col", axis=2, tiled=True)


def body(ancestor_inverse, panel, diag_inverse, structure, block_slot):
    highest = lax.Precision.HIGHEST
    row_count = lax.axis_size("row")
    col_count = lax.axis_size("col")
    row_index = lax.axis_index("row")
    col_index = lax.axis_index("col")
    node_count, slot_count, sub_rows, block_width = panel.shape
    total_slots = slot_count * row_count
    col_slots = total_slots // col_count
    slot_range = jnp.arange(total_slots, dtype=jnp.int32)
    lookup = (structure[:, :, None] == slot_range[None, None, :]).astype(jnp.int32)
    slot_ids = jnp.sum(lookup * block_slot[None, None, :], axis=2)
    chosen = jnp.any(slot_ids[:, :, None] == slot_range[None, None, :], axis=1).astype(jnp.int32)
    local_mask = lax.dynamic_slice_in_dim(chosen, row_index * slot_count, slot_count, 1)
    weight_mask = local_mask.astype(jnp.float32)[:, :, None, None]
    normalized = jnp.einsum("sqik,skw->sqiw", panel, diag_inverse, precision=highest) * weight_mask
    first_slot = col_index * col_slots
    owner_row = first_slot // slot_count
    row_panel = gather_rows(normalized)
    picked = lax.dynamic_slice_in_dim(row_panel, first_slot % slot_count, col_slots, 1)
    column_panel = spread(picked, "row", owner_row)
    column_rows = column_panel.reshape(node_count, col_slots * block_width, block_width)
    leading = jnp.einsum("sij,sik->sjk", diag_inverse, diag_inverse, precision=highest)
    partial_value = jnp.einsum("rc,scw->srw", ancestor_inverse, column_rows, precision=highest)
    partial_value = partial_value.reshape(node_count, slot_count, block_width, block_width)
    product = lax.psum_scatter(partial_value, "col", scatter_dimension=2, tiled=True) * weight_mask
    diag_terms = jnp.einsum("saiw,saiv->swv", normalized, product, precision=highest)
    diag_sum = lax.psum(diag_terms, ("row", "col"))
    return (-product, leading + diag_sum)


def solution(mesh):
    in_specs = (P("row", "col"), P(None, "row", "col", None), P(), P(), P())
    out_specs = (P(None, "row", "col", None), P())
    return jax.shard_map(body, mesh=mesh, in_specs=in_specs, out_specs=out_specs, check_vma=False)
```

profile of v0, /device:TPU:2, one launch (start us, length us, event | category | flops | bytes accessed | tf_op | source)
XLA Modules:
  0.0 785.4 jit_solution(1780212181948259479)
XLA Ops:
  7.2 0.0 copy-start
  7.2 0.0 all-gather.2.cloned.1.call-start
  7.2 1.1 select_reduce_fusion
  8.3 0.1 fusion.8
  8.4 0.1 dynamic-slice_convert_fusion
  8.5 0.1 copy-done
  8.6 2.8 fusion.3
  11.4 0.0 all-gather.2.cloned.1.call-update
  11.5 0.0 all-reduce.3.cloned.1.call-start
  11.5 132.8 %all-gather.2.cloned.1.call-done = f32[6,8,256,256]{3,2,1,0:T(8,128)} async-done(((f32[6,8,8,256]{3,2,1,0:T(8,128)}), f32[6,8,256,256]{3,2,1,0:T(8,128)}) %all-gather.2.cloned.1.call-update) | async-done | bytes 12582928 | tf_op jit(solution)/shard_map/all_gather | solution.py:13
  144.4 3.8 dynamic-slice_select_fusion
  148.2 3.5 copy.10
  151.7 0.0 all-reduce.3.cloned.1.call-update
  151.7 0.0 reduce-scatter.2.cloned.1.call-start
  151.8 143.7 %all-reduce.3.cloned.1.call-done = f32[6,512,256]{1,2,0:T(8,128)} async-done(((f32[6,512,256]{1,2,0:T(8,128)}), f32[6,512,256]{1,2,0:T(8,128)}) %all-reduce.3.cloned.1.call-update) | async-done | bytes 3145744 | tf_op jit(solution)/shard_map/psum | solution.py:9
  295.5 24.8 %convolution_bitcast_fusion = f32[6,2048,256]{1,2,0:T(8,128)} fusion(f32[6,512,256]{1,2,0:T(8,128)} %all-reduce.3.cloned.1.call-done, f32[2048,512]{1,0:T(8,128)} %param.5), kind=kOutput, calls=%fused_computation | convolution fusion | flops 19327352832 | bytes 19922944 | tf_op jit(solution)/shard_map/rc,scw->srw/dot_general | solution.py:39
  320.3 12.6 %copy.11 = f32[6,2048,256]{2,1,0:T(8,128)} copy(f32[6,2048,256]{1,2,0:T(8,128)} %convolution_bitcast_fusion) | data formatting | bytes 25165824 | tf_op jit(solution)/shard_map/rc,scw->srw/transpose | solution.py:39
  332.9 0.0 copy-start.1
  332.9 0.0 reduce-scatter.2.cloned.1.call-update
  332.9 0.2 all-reduce.5.cloned.1.call-start
  333.1 174.8 %reduce-scatter.2.cloned.1.call-done = f32[6,8,8,256]{3,2,1,0:T(8,128)} async-done(((f32[6,8,256,256]{3,2,1,0:T(8,128)}), f32[6,8,8,256]{3,2,1,0:T(8,128)}) %reduce-scatter.2.cloned.1.call-update) | async-done | bytes 393232 | tf_op jit(solution)/shard_map/reduce_scatter | solution.py:41
  507.9 0.0 copy-done.1
  507.9 0.0 copy-start.2
  507.9 3.8 convolution_bitcast_fusion.1
  511.7 0.0 all-reduce.5.cloned.1.call-update
  511.7 0.0 copy-done.2
  511.7 0.9 multiply_negate_fusion
  512.6 261.1 %all-reduce.5.cloned.1.call-done = f32[6,256,256]{2,1,0:T(8,128)} async-done(((f32[6,256,256]{2,1,0:T(8,128)}), f32[6,256,256]{2,1,0:T(8,128)}) %all-reduce.5.cloned.1.call-update) | async-done | bytes 1572880 | tf_op jit(solution)/shard_map/psum | solution.py:43
  773.7 5.2 convolution_add_fusion
  (1 shorter events, 0.0 us)
Async XLA Ops:
  7.2 1.4 copy-start
  7.2 137.2 %all-gather.2.cloned.1.call-start = ((), (), s32[]{:S(2)}) async-start(), calls=%async_computation.1 | async-start | bytes 12976128 | tf_op jit(solution)/shard_map/all_gather | solution.py:13
  11.5 284.0 %all-reduce.3.cloned.1.call-start = ((), (), s32[]{:S(2)}) async-start(), calls=%async_computation.2 | async-start | bytes 6291456 | tf_op jit(solution)/shard_map/psum | solution.py:9
  151.7 356.2 %reduce-scatter.2.cloned.1.call-start = ((), (), s32[]{:S(2)}) async-start(), calls=%async_computation.3 | async-start | bytes 12976128 | tf_op jit(solution)/shard_map/reduce_scatter | solution.py:41
  332.9 175.0 %copy-start.1 = (f32[6,8,8,256]{3,2,1,0:T(8,128)S(1)}, f32[6,8,8,256]{3,2,1,0:T(8,128)}, u32[]{:S(2)}) copy-start(f32[6,8,8,256]{3,2,1,0:T(8,128)} %fusion.3) | copy-start | bytes 1179652
  332.9 440.8 %all-reduce.5.cloned.1.call-start = ((), (), s32[]{:S(2)}) async-start(), calls=%async_computation.4 | async-start | bytes 3145728 | tf_op jit(solution)/shard_map/psum | solution.py:43
  507.9 3.8 copy-start.2
Sparse Core Ops, SparseCore 0:
  11.6 132.7 all-gather.1
  151.8 143.6 all-reduce.2
  333.0 174.8 reduce-scatter.1
  513.7 259.9 all-reduce.4
where the time goes:
time: 786 us; the launch traced here: 785 us
  waiting for transfers between devices  712 us (91%)
  matrix products  36.6 us (5%)
  local copies, waits for them, and re-layouts  16.3 us (2%)
  between operations  13.8 us (2%)
    psum x1, waiting for transfers between devices, body(): diag_sum = lax.psum(diag_terms, ('row', 'col'))  261 us
    reduce_scatter x1, waiting for transfers between devices, body(): lax.psum_scatter(partial_value, 'col', scatter_dimension=2, tiled=True)  175 us
    psum x1, waiting for transfers between devices, spread(): return lax.psum(block, axis)  144 us
    all_gather x1, waiting for transfers between devices, gather_rows(): return lax.all_gather(normalized, 'col', axis=2, tiled=True)  133 us
    dot_general x1, matrix products, body(): jnp.einsum('rc,scw->srw', ancestor_inverse, column_rows, precision=highest)  24.8 us
  transfers between devices with their start and end apart: 4, of which 4 were waited for; matrix products, arithmetic and copies ran while one was open for 0% of the time, Pallas kernels for 0%

commit v1 on v0

--- a/solution.py
+++ b/solution.py
@@ -40,7 +40,9 @@
     partial_value = partial_value.reshape(node_count, slot_count, block_width, block_width)
     product = lax.psum_scatter(partial_value, "col", scatter_dimension=2, tiled=True) * weight_mask
     diag_terms = jnp.einsum("saiw,saiv->swv", normalized, product, precision=highest)
-    diag_sum = lax.psum(diag_terms, ("row", "col"))
+    diag_sum = diag_terms
+    for over in ("row", "col"):
+        diag_sum = lax.psum(diag_sum, over)
     return (-product, leading + diag_sum)
 
 

time: 786 us -> 893 us (1.14)
  waiting for transfers between devices: 712 us -> 818 us
    psum x1 -> x2, waiting for transfers between devices: 261 us -> 367 us  [body(): diag_sum = lax.psum(diag_sum, over)]
  transfers between devices with their start and end apart: 4 -> 5, of which waited for: 4 -> 5; matrix products, arithmetic and copies ran while one was open for 0% -> 0% of each run, Pallas kernels for 0% -> 0%
where the time goes in v1:
time: 893 us; the launch traced here: 891 us
  waiting for transfers between devices  818 us (92%)
  matrix products  36.7 us (4%)
  local copies, waits for them, and re-layouts  16.3 us (2%)
  between operations  13.8 us (2%)
    psum x2, waiting for transfers between devices, body(): diag_sum = lax.psum(diag_sum, over)  367 us
    reduce_scatter x1, waiting for transfers between devices, body(): lax.psum_scatter(partial_value, 'col', scatter_dimension=2, tiled=True)  175 us
    psum x1, waiting for transfers between devices, spread(): return lax.psum(block, axis)  144 us
    all_gather x1, waiting for transfers between devices, gather_rows(): return lax.all_gather(normalized, 'col', axis=2, tiled=True)  133 us
    dot_general x1, matrix products, body(): jnp.einsum('rc,scw->srw', ancestor_inverse, column_rows, precision=highest)  24.8 us
  transfers between devices with their start and end apart: 5, of which 5 were waited for; matrix products, arithmetic and copies ran while one was open for 0% of the time, Pallas kernels for 0%

profile of v1, /device:TPU:2, one launch (start us, length us, event | category | flops | bytes accessed | tf_op | source)
XLA Modules:
  0.0 891.2 jit_solution(17210796001445058578)
XLA Ops:
  7.2 0.0 copy-start
  7.2 0.0 all-gather.2.cloned.1.call-start
  7.2 1.1 select_reduce_fusion
  8.3 0.1 fusion.8
  8.4 0.1 dynamic-slice_convert_fusion
  8.5 0.1 copy-done
  8.6 2.8 fusion.3
  11.4 0.0 all-gather.2.cloned.1.call-update
  11.5 0.0 all-reduce.4.cloned.1.call-start
  11.5 132.8 %all-gather.2.cloned.1.call-done = f32[6,8,256,256]{3,2,1,0:T(8,128)} async-done(((f32[6,8,8,256]{3,2,1,0:T(8,128)}), f32[6,8,256,256]{3,2,1,0:T(8,128)}) %all-gather.2.cloned.1.call-update) | async-done | bytes 12582928 | tf_op jit(solution)/shard_map/all_gather | solution.py:13
  144.4 3.8 dynamic-slice_select_fusion
  148.2 3.5 copy.10
  151.7 0.0 all-reduce.4.cloned.1.call-update
  151.7 0.0 reduce-scatter.2.cloned.1.call-start
  151.8 143.7 %all-reduce.4.cloned.1.call-done = f32[6,512,256]{1,2,0:T(8,128)} async-done(((f32[6,512,256]{1,2,0:T(8,128)}), f32[6,512,256]{1,2,0:T(8,128)}) %all-reduce.4.cloned.1.call-update) | async-done | bytes 3145744 | tf_op jit(solution)/shard_map/psum | solution.py:9
  295.5 24.8 %convolution_bitcast_fusion = f32[6,2048,256]{1,2,0:T(8,128)} fusion(f32[6,512,256]{1,2,0:T(8,128)} %all-reduce.4.cloned.1.call-done, f32[2048,512]{1,0:T(8,128)} %param.5), kind=kOutput, calls=%fused_computation | convolution fusion | flops 19327352832 | bytes 19922944 | tf_op jit(solution)/shard_map/rc,scw->srw/dot_general | solution.py:39
  320.3 12.6 %copy.11 = f32[6,2048,256]{2,1,0:T(8,128)} copy(f32[6,2048,256]{1,2,0:T(8,128)} %convolution_bitcast_fusion) | data formatting | bytes 25165824 | tf_op jit(solution)/shard_map/rc,scw->srw/transpose | solution.py:39
  332.9 0.0 copy-start.1
  332.9 0.0 reduce-scatter.2.cloned.1.call-update
  332.9 0.0 all-reduce.6.cloned.1.call-start
  332.9 174.9 %reduce-scatter.2.cloned.1.call-done = f32[6,8,8,256]{3,2,1,0:T(8,128)} async-done(((f32[6,8,256,256]{3,2,1,0:T(8,128)}), f32[6,8,8,256]{3,2,1,0:T(8,128)}) %reduce-scatter.2.cloned.1.call-update) | async-done | bytes 393232 | tf_op jit(solution)/shard_map/reduce_scatter | solution.py:41
  507.9 0.0 copy-done.1
  507.9 0.0 copy-start.2
  507.9 3.8 convolution_bitcast_fusion.1
  511.7 0.0 all-reduce.6.cloned.1.call-update
  511.7 0.2 all-reduce.8.cloned.1.call-start
  512.0 90.8 %all-reduce.6.cloned.1.call-done = f32[6,256,256]{2,1,0:T(8,128)} async-done(((f32[6,256,256]{2,1,0:T(8,128)}), f32[6,256,256]{2,1,0:T(8,128)}) %all-reduce.6.cloned.1.call-update) | async-done | bytes 1572880 | tf_op jit(solution)/shard_map/psum | solution.py:45
  602.8 0.0 all-reduce.8.cloned.1.call-update
  602.8 0.0 copy-done.2
  602.8 0.9 multiply_negate_fusion
  603.7 275.8 %all-reduce.8.cloned.1.call-done = f32[6,256,256]{2,1,0:T(8,128)} async-done(((f32[6,256,256]{2,1,0:T(8,128)}), f32[6,256,256]{2,1,0:T(8,128)}) %all-reduce.8.cloned.1.call-update) | async-done | bytes 1572880 | tf_op jit(solution)/shard_map/psum | solution.py:45
  879.4 5.2 convolution_add_fusion
  (1 shorter events, 0.0 us)
Async XLA Ops:
  7.2 1.4 copy-start
  7.2 137.2 %all-gather.2.cloned.1.call-start = ((), (), s32[]{:S(2)}) async-start(), calls=%async_computation.1 | async-start | bytes 12976128 | tf_op jit(solution)/shard_map/all_gather | solution.py:13
  11.5 284.0 %all-reduce.4.cloned.1.call-start = ((), (), s32[]{:S(2)}) async-start(), calls=%async_computation.2 | async-start | bytes 6291456 | tf_op jit(solution)/shard_map/psum | solution.py:9
  151.7 356.2 %reduce-scatter.2.cloned.1.call-start = ((), (), s32[]{:S(2)}) async-start(), calls=%async_computation.3 | async-start | bytes 12976128 | tf_op jit(solution)/shard_map/reduce_scatter | solution.py:41
  332.9 175.0 %copy-start.1 = (f32[6,8,8,256]{3,2,1,0:T(8,128)S(1)}, f32[6,8,8,256]{3,2,1,0:T(8,128)}, u32[]{:S(2)}) copy-start(f32[6,8,8,256]{3,2,1,0:T(8,128)} %fusion.3) | copy-start | bytes 1179652
  332.9 269.9 %all-reduce.6.cloned.1.call-start = ((), (), s32[]{:S(2)}) async-start(), calls=%async_computation.4 | async-start | bytes 3145728 | tf_op jit(solution)/shard_map/psum | solution.py:45
  507.9 94.9 %copy-start.2 = (f32[6,8,8,256]{3,2,1,0:T(8,128)S(1)}, f32[6,8,8,256]{3,2,1,0:T(8,128)}, u32[]{:S(2)}) copy-start(f32[6,8,8,256]{3,2,1,0:T(8,128)} %reduce-scatter.2.cloned.1.call-done) | copy-start | bytes 1179652
  511.7 367.7 %all-reduce.8.cloned.1.call-start = ((), (), s32[]{:S(2)}) async-start(), calls=%async_computation.5 | async-start | bytes 3145728 | tf_op jit(solution)/shard_map/psum | solution.py:45
Sparse Core Ops, SparseCore 0:
  11.6 132.7 all-gather.1
  151.8 143.6 all-reduce.3
  333.0 174.8 reduce-scatter.1
  511.8 90.8 all-reduce.5
  605.2 274.1 all-reduce.7
